TPU v7x, 128 devices: a whole 4x4x4 slice. The times are simulated.
128 devices in a mesh: probe: 4 (over z_hi, core), sx: 4 (over x), sy: 8 (over y, z_lo).
Axes of the slice: x: 4, y: 4, z: 4 (z_hi: 2, z_lo: 2; z = z_hi * 2 + z_lo), core: 2. Of those that a mesh axis runs over, the one named last changes fastest.
Arguments:
- probes: float32 [8, 128, 256, 256], P('probe', 'sx', 'sy'), may hold values from -6 to 6
- velocity: float32 [3, 128, 256, 256], P(None, 'sx', 'sy'), may hold values from -0.15 to 0.15
- diffusivity: float32 [128, 256, 256], P('sx', 'sy'), may hold values from 0.02 to 0.15
- obs_weight: float32 [128, 256, 256], P('sx', 'sy'), may hold values from 0.05 to 1
Outputs:
- basis_fields: float32 [8, 128, 256, 256], P('probe', 'sx', 'sy')
- projected_hessian: float32 [8, 8], replicated
All inputs are finite; a program needn't handle non-finite values.
Results may differ from a plain program's by a relative error of at most 0.00013.
Values sent between devices are 32-bit elements; how exact they have to be, the bound alone decides.
A program may use at most 128 MiB of HBM per device.

v0:
```python
import jax
import jax.numpy as jnp
from jax import lax
from jax.sharding import PartitionSpec as P

STEPS = 4


def extended(value, sides, width):
    for axis, dim in sides:
        devices, length = (lax.axis_size(axis), value.shape[dim])
        up = [(i, (i + 1) % devices) for i in range(devices - 1)]
        down = [(j, i) for i, j in up]
        last = lax.slice_in_dim(value, length - width, length, axis=dim)
        leading = lax.slice_in_dim(value, 0, width, axis=dim)
        before = lax.ppermute(last, axis, up)
        after = lax.ppermute(leading, axis, down)
        value = jnp.concatenate([before, value, after], axis=dim)
    return value


def forward_step(state, coeffs):
    cc = coeffs[:, 1:-1, 1:-1, :]
    spread = cc[0]
    inner = state[:, 1:-1, 1:-1, :]
    padded = jnp.pad(inner, ((0, 0), (0, 0), (0, 0), (1, 1)))
    result = (1.0 - 6.0 * spread) * inner
    result = (
        result
        + (spread - 0.5 * cc[1]) * state[:, 2:, 1:-1, :]
        + (spread + 0.5 * cc[1]) * state[:, :-2, 1:-1, :]
    )
    result = (
        result
        + (spread - 0.5 * cc[2]) * state[:, 1:-1, 2:, :]
        + (spread + 0.5 * cc[2]) * state[:, 1:-1, :-2, :]
    )
    result = (
        result
        + (spread - 0.5 * cc[3]) * padded[..., 2:]
        + (spread + 0.5 * cc[3]) * padded[..., :-2]
    )
    return result


def adjoint_step(state, coeffs):
    spread = coeffs[0]
    plus_x = (spread - 0.5 * coeffs[1]) * state
    minus_x = (spread + 0.5 * coeffs[1]) * state
    plus_y = (spread - 0.5 * coeffs[2]) * state
    minus_y = (spread + 0.5 * coeffs[2]) * state
    cc = coeffs[:, 1:-1, 1:-1, :]
    inner = state[:, 1:-1, 1:-1, :]
    pad_plus = jnp.pad((cc[0] - 0.5 * cc[3]) * inner, ((0, 0), (0, 0), (0, 0), (1, 1)))
    pad_minus = jnp.pad((cc[0] + 0.5 * cc[3]) * inner, ((0, 0), (0, 0), (0, 0), (1, 1)))
    result = (1.0 - 6.0 * cc[0]) * inner
    result = result + plus_x[:, :-2, 1:-1, :] + minus_x[:, 2:, 1:-1, :]
    result = result + plus_y[:, 1:-1, :-2, :] + minus_y[:, 1:-1, 2:, :]
    result = result + pad_plus[..., :-2] + pad_minus[..., 2:]
    return result


def factor_inverse(gram, count):
    lower = jnp.linalg.cholesky(gram)
    return jax.scipy.linalg.solve_triangular(lower, jnp.eye(count, dtype=jnp.float32), lower=True)


def shards(probes, velocity, diffusivity, obs_weight):
    group = probes.shape[0]
    count = group * lax.axis_size("probe")
    ncells = (
        probes.shape[1]
        * probes.shape[2]
        * probes.shape[3]
        * lax.axis_size("sx")
        * lax.axis_size("sy")
    )
    coeffs = jnp.concatenate([diffusivity[None], velocity], axis=0)
    highest = lax.Precision.HIGHEST
    edge_coeffs = extended(coeffs, (("sx", 1), ("sy", 2)), 1)

    def forward(state):
        for step in range(STEPS):
            padded = extended(state, (("sx", 1), ("sy", 2)), 1)
            state = forward_step(padded, edge_coeffs)
        return state

    state = obs_weight * forward(probes)
    for step in range(STEPS):
        padded = extended(state, (("sx", 1), ("sy", 2)), 1)
        state = adjoint_step(padded, edge_coeffs)
    images = state
    again = forward(images)
    root = jnp.sqrt(obs_weight) * again
    both = jnp.stack([images, root], axis=1)
    slabs = lax.all_to_all(both, "probe", split_axis=2, concat_axis=0, tiled=True)
    flat = slabs[:, 0].reshape(count, -1)
    flat_root = slabs[:, 1].reshape(count, -1)
    partial_gram = jnp.dot(flat, flat.T, precision=highest)
    partial_cross = jnp.dot(flat_root, flat_root.T, precision=highest)
    sums = lax.psum(jnp.stack([partial_gram, partial_cross]), ("probe", "sx", "sy")) / ncells
    gram, cross = (sums[0], sums[1])
    inverse = factor_inverse(gram, count)
    basis_slab = jnp.dot(inverse, flat, precision=highest)
    basis_fields = lax.all_to_all(
        basis_slab.reshape(slabs[:, 0].shape), "probe", split_axis=0, concat_axis=1, tiled=True
    )
    projected = jnp.dot(jnp.dot(inverse, cross, precision=highest), inverse.T, precision=highest)
    return (basis_fields, projected)


def solution(mesh):
    return jax.shard_map(
        shards,
        mesh=mesh,
        in_specs=(
            P("probe", "sx", "sy", None),
            P(None, "sx", "sy", None),
            P("sx", "sy", None),
            P("sx", "sy", None),
        ),
        out_specs=(P("probe", "sx", "sy", None), P()),
        check_vma=False,
    )
```

profile of v0, /device:TPU:1, one launch (start us, length us, event | category | flops | bytes accessed | tf_op | source)
XLA Modules:
  0.0 471.6 jit_solution(13638757533432052887)
XLA Ops:
  3.0 4.6 collective-permute-start.1
  12.0 4.4 collective-permute-start.3
  21.8 3.5 fusion.10
  26.7 4.0 collective-permute-start.5
  33.3 4.9 %collective-permute-start.7 = (f32[2,34,1,256]{3,1,2,0:T(8,128)S(1)}, f32[2,34,1,256]{3,1,2,0:T(8,128)S(1)}, u32[]{:S(2)}, u32[]{:S(2)}) collective-permute-start(f32[2,34,1,256]{3,1,2,0:T(8,128)S(1)} %get-tuple-element.46), channel_id=1, source_target_pairs={{0,1},{1,2},{2,3},{3,4},{4,5},{5,6},{6,7},{8,9},{9,10},{10,11},{11... | collective-permute-start | bytes 208904 | tf_op jit(solution)/shard_map/ppermute | solution.py:16
  38.3 4.0 collective-permute-start.16
  43.6 3.5 fusion.14
  48.4 4.6 collective-permute-start.9
  53.3 4.4 collective-permute-start.18
  60.4 4.8 %collective-permute-start.11 = (f32[2,34,1,256]{3,1,2,0:T(8,128)S(1)}, f32[2,34,1,256]{3,1,2,0:T(8,128)S(1)}, u32[]{:S(2)}, u32[]{:S(2)}) collective-permute-start(f32[2,34,1,256]{3,1,2,0:T(8,128)S(1)} %get-tuple-element.44), channel_id=1, source_target_pairs={{0,1},{1,2},{2,3},{3,4},{4,5},{5,6},{6,7},{8,9},{9,10},{10,11},{11... | collective-permute-start | bytes 208904 | tf_op jit(solution)/shard_map/ppermute | solution.py:16
  68.3 3.4 fusion.18
  73.1 4.3 collective-permute-start.13
  80.0 4.4 collective-permute-start.15
  85.9 3.5 broadcast_multiply_fusion.3
  89.6 3.7 collective-permute-start.20
  98.3 4.3 collective-permute-start.22
  105.5 3.5 collective-permute-done.23
  109.5 3.9 broadcast_multiply_fusion.2
  113.5 3.5 collective-permute-start.24
  118.4 3.7 collective-permute-done.25
  122.1 4.3 collective-permute-start.26
  132.0 3.9 broadcast_multiply_fusion.1
  140.7 3.9 collective-permute-done.29
  149.4 3.5 collective-permute-done.31
  153.3 3.7 broadcast_multiply_fusion
  161.4 3.7 collective-permute-done.33
  165.1 4.3 collective-permute-start.34
  171.1 3.4 collective-permute-done.35
  179.1 4.0 collective-permute-start.37
  185.8 4.0 collective-permute-start.39
  192.0 3.4 fusion.27
  196.8 4.0 collective-permute-start.41
  203.5 4.4 collective-permute-start.43
  210.5 3.4 fusion.31
  215.3 4.4 collective-permute-start.45
  222.4 4.4 collective-permute-start.47
  233.2 4.6 collective-permute-start.49
  240.4 5.3 %collective-permute-start.51 = (f32[2,34,1,256]{3,1,2,0:T(8,128)S(1)}, f32[2,34,1,256]{3,1,2,0:T(8,128)S(1)}, u32[]{:S(2)}, u32[]{:S(2)}) collective-permute-start(f32[2,34,1,256]{3,1,2,0:T(8,128)S(1)} %get-tuple-element.26), channel_id=1, source_target_pairs={{0,1},{1,2},{2,3},{3,4},{4,5},{5,6},{6,7},{8,9},{9,10},{10,11},{11... | collective-permute-start | bytes 208904 | tf_op jit(solution)/shard_map/ppermute | solution.py:16
  247.1 3.5 fusion.41
  253.3 79.6 %all_to_all.36 = f32[2,2,32,32,256]{4,3,0,1,2:T(8,128)S(1)} all-to-all(f32[2,2,32,32,256]{4,3,0,1,2:T(8,128)S(1)} %copy.58), channel_id=1, replica_groups=mesh['probe'=4,'sx'=4,'sy'=8] {'probe'}, dimensions={2} | all-to-all | bytes 8388608 | tf_op jit(solution)/shard_map/all_to_all | solution.py:96
  333.0 5.2 %copy.72 = f32[2,2,4,8,32,256]{5,0,2,4,3,1:T(2,128)} copy(f32[2,2,4,8,32,256]{5,4,0,1,3,2:T(8,128)S(1)} %bitcast.90) | data formatting | bytes 8388608 | tf_op jit(solution)/shard_map/all_to_all | solution.py:96
  338.2 6.1 %all_to_all.29 = f32[8,2,8,32,256]{4,0,3,2,1:T(8,128)} reshape(f32[4,2,2,8,32,256]{5,1,0,4,3,2:T(2,128)} %bitcast.91) | data formatting | bytes 8388608 | tf_op jit(solution)/shard_map/all_to_all | solution.py:96
  344.4 7.1 %fusion.131 = f32[1,8,8]{2,1,0:T(8,128)S(1)} fusion(f32[8,2,8,32,256]{4,0,3,2,1:T(8,128)} %all_to_all.29), kind=kOutput, calls=%fused_computation.253 | convolution fusion | flops 50331648 | bytes 2097408 | tf_op jit(solution)/shard_map/dot_general | solution.py:99
  351.5 7.1 %fusion.134 = f32[1,8,8]{2,1,0:T(8,128)S(1)} fusion(f32[8,2,8,32,256]{4,0,3,2,1:T(8,128)} %all_to_all.29), kind=kOutput, calls=%fused_computation.254 | convolution fusion | flops 50331648 | bytes 2097408 | tf_op jit(solution)/shard_map/dot_general | solution.py:100
  358.6 72.6 %psum.7 = f32[2,8,8]{2,1,0:T(8,128)S(1)} all-reduce(f32[2,8,8]{2,1,0:T(8,128)S(1)} %pad_maximum_fusion.117), channel_id=1, replica_groups=mesh['probe'=4,'sx'=4,'sy'=8] {'probe','sx','sy'}, use_global_device_ids=true, to_apply=%region_0.1 | all-reduce | flops 128 | bytes 1024 | tf_op jit(solution)/shard_map/psum | solution.py:101
  434.2 3.4 fusion.124
  439.6 4.1 all-to-all-start.1
  444.6 25.3 %all-to-all-done.1 = f32[8,8,32,256]{3,2,1,0:T(8,128)S(1)} async-done(((f32[8,8,32,256]{3,2,1,0:T(8,128)}), f32[8,8,32,256]{3,2,1,0:T(8,128)S(1)}, u32[]{:S(2)}, u32[]{:S(2)}) %all-to-all-start.1) | async-done | bytes 2097184 | tf_op jit(solution)/shard_map/all_to_all | solution.py:105
  (167 shorter events, 101.8 us)
Async XLA Ops:
  1.6 8.9 %collective-permute-start = (f32[2,1,32,256]{3,1,2,0:T(1,128)S(1)}, f32[2,1,32,256]{3,1,2,0:T(1,128)S(1)}, u32[]{:S(2)}, u32[]{:S(2)}) collective-permute-start(f32[2,1,32,256]{3,1,2,0:T(1,128)S(1)} %copy.38), channel_id=1, source_target_pairs={{8,0},{16,8},{24,16},{9,1},{17,9},{25,17},{10,2},{18,10},{26,18},{... | collective-permute-start | bytes 196616 | tf_op jit(solution)/shard_map/ppermute | solution.py:17
  3.0 7.6 %collective-permute-start.1 = (f32[2,1,32,256]{3,1,2,0:T(1,128)S(1)}, f32[2,1,32,256]{3,1,2,0:T(1,128)S(1)}, u32[]{:S(2)}, u32[]{:S(2)}) collective-permute-start(f32[2,1,32,256]{3,1,2,0:T(1,128)S(1)} %copy.41), channel_id=1, source_target_pairs={{0,8},{8,16},{16,24},{1,9},{9,17},{17,25},{2,10},{10,18},{18,26},{... | collective-permute-start | bytes 196616 | tf_op jit(solution)/shard_map/ppermute | solution.py:16
  10.6 11.2 %collective-permute-start.2 = (f32[2,34,1,256]{3,1,2,0:T(8,128)S(1)}, f32[2,34,1,256]{3,1,2,0:T(8,128)S(1)}, u32[]{:S(2)}, u32[]{:S(2)}) collective-permute-start(f32[2,34,1,256]{3,1,2,0:T(8,128)S(1)} %get-tuple-element.47), channel_id=1, source_target_pairs={{1,0},{2,1},{3,2},{4,3},{5,4},{6,5},{7,6},{9,8},{10,9},{11,10},{12... | collective-permute-start | bytes 208904 | tf_op jit(solution)/shard_map/ppermute | solution.py:17
  12.0 9.8 %collective-permute-start.3 = (f32[2,34,1,256]{3,1,2,0:T(8,128)S(1)}, f32[2,34,1,256]{3,1,2,0:T(8,128)S(1)}, u32[]{:S(2)}, u32[]{:S(2)}) collective-permute-start(f32[2,34,1,256]{3,1,2,0:T(8,128)S(1)} %get-tuple-element.48), channel_id=1, source_target_pairs={{0,1},{1,2},{2,3},{3,4},{4,5},{5,6},{6,7},{8,9},{9,10},{10,11},{11... | collective-permute-start | bytes 208904 | tf_op jit(solution)/shard_map/ppermute | solution.py:16
  25.4 5.3 %collective-permute-start.4 = (f32[2,1,32,256]{3,1,2,0:T(1,128)S(1)}, f32[2,1,32,256]{3,1,2,0:T(1,128)S(1)}, u32[]{:S(2)}, u32[]{:S(2)}) collective-permute-start(f32[2,1,32,256]{3,1,2,0:T(1,128)S(1)} %get-tuple-element.70), channel_id=1, source_target_pairs={{8,0},{16,8},{24,16},{9,1},{17,9},{25,17},{10,2},{18,10},{26,18},{... | collective-permute-start | bytes 196616 | tf_op jit(solution)/shard_map/ppermute | solution.py:17
  26.7 5.3 %collective-permute-start.5 = (f32[2,1,32,256]{3,1,2,0:T(1,128)S(1)}, f32[2,1,32,256]{3,1,2,0:T(1,128)S(1)}, u32[]{:S(2)}, u32[]{:S(2)}) collective-permute-start(f32[2,1,32,256]{3,1,2,0:T(1,128)S(1)} %get-tuple-element.69), channel_id=1, source_target_pairs={{0,8},{8,16},{16,24},{1,9},{9,17},{17,25},{2,10},{10,18},{18,26},{... | collective-permute-start | bytes 196616 | tf_op jit(solution)/shard_map/ppermute | solution.py:16
  32.0 11.5 %collective-permute-start.6 = (f32[2,34,1,256]{3,1,2,0:T(8,128)S(1)}, f32[2,34,1,256]{3,1,2,0:T(8,128)S(1)}, u32[]{:S(2)}, u32[]{:S(2)}) collective-permute-start(f32[2,34,1,256]{3,1,2,0:T(8,128)S(1)} %get-tuple-element.45), channel_id=1, source_target_pairs={{1,0},{2,1},{3,2},{4,3},{5,4},{6,5},{7,6},{9,8},{10,9},{11,10},{12... | collective-permute-start | bytes 208904 | tf_op jit(solution)/shard_map/ppermute | solution.py:17
  33.3 10.2 %collective-permute-start.7 = (f32[2,34,1,256]{3,1,2,0:T(8,128)S(1)}, f32[2,34,1,256]{3,1,2,0:T(8,128)S(1)}, u32[]{:S(2)}, u32[]{:S(2)}) collective-permute-start(f32[2,34,1,256]{3,1,2,0:T(8,128)S(1)} %get-tuple-element.46), channel_id=1, source_target_pairs={{0,1},{1,2},{2,3},{3,4},{4,5},{5,6},{6,7},{8,9},{9,10},{10,11},{11... | collective-permute-start | bytes 208904 | tf_op jit(solution)/shard_map/ppermute | solution.py:16
  38.3 14.8 %collective-permute-start.16 = (f32[4,1,32,256]{3,2,1,0:T(8,128)S(1)}, f32[4,1,32,256]{3,2,1,0:T(8,128)S(1)}, u32[]{:S(2)}, u32[]{:S(2)}) collective-permute-start(f32[4,1,32,256]{3,2,1,0:T(8,128)S(1)} %get-tuple-element.17), channel_id=1, source_target_pairs={{0,8},{8,16},{16,24},{1,9},{9,17},{17,25},{2,10},{10,18},{18,26},{... | collective-permute-start | bytes 393224 | tf_op jit(solution)/shard_map/ppermute | solution.py:16
  42.3 10.8 %collective-permute-start.17 = (f32[4,1,32,256]{3,2,1,0:T(8,128)S(1)}, f32[4,1,32,256]{3,2,1,0:T(8,128)S(1)}, u32[]{:S(2)}, u32[]{:S(2)}) collective-permute-start(f32[4,1,32,256]{3,2,1,0:T(8,128)S(1)} %get-tuple-element.18), channel_id=1, source_target_pairs={{8,0},{16,8},{24,16},{9,1},{17,9},{25,17},{10,2},{18,10},{26,18},{... | collective-permute-start | bytes 393224 | tf_op jit(solution)/shard_map/ppermute | solution.py:17
  47.1 11.9 %collective-permute-start.8 = (f32[2,1,32,256]{3,1,2,0:T(1,128)S(1)}, f32[2,1,32,256]{3,1,2,0:T(1,128)S(1)}, u32[]{:S(2)}, u32[]{:S(2)}) collective-permute-start(f32[2,1,32,256]{3,1,2,0:T(1,128)S(1)} %get-tuple-element.68), channel_id=1, source_target_pairs={{8,0},{16,8},{24,16},{9,1},{17,9},{25,17},{10,2},{18,10},{26,18},{... | collective-permute-start | bytes 196616 | tf_op jit(solution)/shard_map/ppermute | solution.py:17
  48.4 10.6 %collective-permute-start.9 = (f32[2,1,32,256]{3,1,2,0:T(1,128)S(1)}, f32[2,1,32,256]{3,1,2,0:T(1,128)S(1)}, u32[]{:S(2)}, u32[]{:S(2)}) collective-permute-start(f32[2,1,32,256]{3,1,2,0:T(1,128)S(1)} %get-tuple-element.67), channel_id=1, source_target_pairs={{0,8},{8,16},{16,24},{1,9},{9,17},{17,25},{2,10},{10,18},{18,26},{... | collective-permute-start | bytes 196616 | tf_op jit(solution)/shard_map/ppermute | solution.py:16
  53.3 12.5 %collective-permute-start.18 = (f32[4,34,1,256]{3,1,2,0:T(8,128)S(1)}, f32[4,34,1,256]{3,1,2,0:T(8,128)S(1)}, u32[]{:S(2)}, u32[]{:S(2)}) collective-permute-start(f32[4,34,1,256]{3,1,2,0:T(8,128)S(1)} %copy.49), channel_id=1, source_target_pairs={{0,1},{1,2},{2,3},{3,4},{4,5},{5,6},{6,7},{8,9},{9,10},{10,11},{11... | collective-permute-start | bytes 417800 | tf_op jit(solution)/shard_map/ppermute | solution.py:16
  57.8 8.2 %collective-permute-start.19 = (f32[4,34,1,256]{3,1,2,0:T(8,128)S(1)}, f32[4,34,1,256]{3,1,2,0:T(8,128)S(1)}, u32[]{:S(2)}, u32[]{:S(2)}) collective-permute-start(f32[4,34,1,256]{3,1,2,0:T(8,128)S(1)} %copy.50), channel_id=1, source_target_pairs={{1,0},{2,1},{3,2},{4,3},{5,4},{6,5},{7,6},{9,8},{10,9},{11,10},{12... | collective-permute-start | bytes 417800 | tf_op jit(solution)/shard_map/ppermute | solution.py:17
  59.1 7.1 %collective-permute-start.10 = (f32[2,34,1,256]{3,1,2,0:T(8,128)S(1)}, f32[2,34,1,256]{3,1,2,0:T(8,128)S(1)}, u32[]{:S(2)}, u32[]{:S(2)}) collective-permute-start(f32[2,34,1,256]{3,1,2,0:T(8,128)S(1)} %get-tuple-element.43), channel_id=1, source_target_pairs={{1,0},{2,1},{3,2},{4,3},{5,4},{6,5},{7,6},{9,8},{10,9},{11,10},{12... | collective-permute-start | bytes 208904 | tf_op jit(solution)/shard_map/ppermute | solution.py:17
  60.4 7.9 %collective-permute-start.11 = (f32[2,34,1,256]{3,1,2,0:T(8,128)S(1)}, f32[2,34,1,256]{3,1,2,0:T(8,128)S(1)}, u32[]{:S(2)}, u32[]{:S(2)}) collective-permute-start(f32[2,34,1,256]{3,1,2,0:T(8,128)S(1)} %get-tuple-element.44), channel_id=1, source_target_pairs={{0,1},{1,2},{2,3},{3,4},{4,5},{5,6},{6,7},{8,9},{9,10},{10,11},{11... | collective-permute-start | bytes 208904 | tf_op jit(solution)/shard_map/ppermute | solution.py:16
  71.8 6.1 %collective-permute-start.12 = (f32[2,1,32,256]{3,1,2,0:T(1,128)S(1)}, f32[2,1,32,256]{3,1,2,0:T(1,128)S(1)}, u32[]{:S(2)}, u32[]{:S(2)}) collective-permute-start(f32[2,1,32,256]{3,1,2,0:T(1,128)S(1)} %get-tuple-element.66), channel_id=1, source_target_pairs={{8,0},{16,8},{24,16},{9,1},{17,9},{25,17},{10,2},{18,10},{26,18},{... | collective-permute-start | bytes 196616 | tf_op jit(solution)/shard_map/ppermute | solution.py:17
  73.1 5.6 %collective-permute-start.13 = (f32[2,1,32,256]{3,1,2,0:T(1,128)S(1)}, f32[2,1,32,256]{3,1,2,0:T(1,128)S(1)}, u32[]{:S(2)}, u32[]{:S(2)}) collective-permute-start(f32[2,1,32,256]{3,1,2,0:T(1,128)S(1)} %get-tuple-element.65), channel_id=1, source_target_pairs={{0,8},{8,16},{16,24},{1,9},{9,17},{17,25},{2,10},{10,18},{18,26},{... | collective-permute-start | bytes 196616 | tf_op jit(solution)/shard_map/ppermute | solution.py:16
  78.7 6.1 %collective-permute-start.14 = (f32[2,34,1,256]{3,1,2,0:T(8,128)S(1)}, f32[2,34,1,256]{3,1,2,0:T(8,128)S(1)}, u32[]{:S(2)}, u32[]{:S(2)}) collective-permute-start(f32[2,34,1,256]{3,1,2,0:T(8,128)S(1)} %get-tuple-element.41), channel_id=1, source_target_pairs={{1,0},{2,1},{3,2},{4,3},{5,4},{6,5},{7,6},{9,8},{10,9},{11,10},{12... | collective-permute-start | bytes 208904 | tf_op jit(solution)/shard_map/ppermute | solution.py:17
  80.0 5.9 %collective-permute-start.15 = (f32[2,34,1,256]{3,1,2,0:T(8,128)S(1)}, f32[2,34,1,256]{3,1,2,0:T(8,128)S(1)}, u32[]{:S(2)}, u32[]{:S(2)}) collective-permute-start(f32[2,34,1,256]{3,1,2,0:T(8,128)S(1)} %get-tuple-element.42), channel_id=1, source_target_pairs={{0,1},{1,2},{2,3},{3,4},{4,5},{5,6},{6,7},{8,9},{9,10},{10,11},{11... | collective-permute-start | bytes 208904 | tf_op jit(solution)/shard_map/ppermute | solution.py:16
  89.6 8.2 %collective-permute-start.20 = (f32[2,1,32,256]{3,1,2,0:T(1,128)S(1)}, f32[2,1,32,256]{3,1,2,0:T(1,128)S(1)}, u32[]{:S(2)}, u32[]{:S(2)}) collective-permute-start(f32[2,1,32,256]{3,1,2,0:T(1,128)S(1)} %get-tuple-element.63), channel_id=1, source_target_pairs={{0,8},{8,16},{16,24},{1,9},{9,17},{17,25},{2,10},{10,18},{18,26},{... | collective-permute-start | bytes 196616 | tf_op jit(solution)/shard_map/ppermute | solution.py:16
  93.3 5.0 %collective-permute-start.21 = (f32[2,1,32,256]{3,1,2,0:T(1,128)S(1)}, f32[2,1,32,256]{3,1,2,0:T(1,128)S(1)}, u32[]{:S(2)}, u32[]{:S(2)}) collective-permute-start(f32[2,1,32,256]{3,1,2,0:T(1,128)S(1)} %get-tuple-element.64), channel_id=1, source_target_pairs={{8,0},{16,8},{24,16},{9,1},{17,9},{25,17},{10,2},{18,10},{26,18},{... | collective-permute-start | bytes 196616 | tf_op jit(solution)/shard_map/ppermute | solution.py:17
  98.3 7.2 %collective-permute-start.22 = (f32[2,34,1,256]{3,1,2,0:T(8,128)S(1)}, f32[2,34,1,256]{3,1,2,0:T(8,128)S(1)}, u32[]{:S(2)}, u32[]{:S(2)}) collective-permute-start(f32[2,34,1,256]{3,1,2,0:T(8,128)S(1)} %get-tuple-element.39), channel_id=1, source_target_pairs={{0,1},{1,2},{2,3},{3,4},{4,5},{5,6},{6,7},{8,9},{9,10},{10,11},{11... | collective-permute-start | bytes 208904 | tf_op jit(solution)/shard_map/ppermute | solution.py:16
  102.6 6.4 %collective-permute-start.23 = (f32[2,34,1,256]{3,1,2,0:T(8,128)S(1)}, f32[2,34,1,256]{3,1,2,0:T(8,128)S(1)}, u32[]{:S(2)}, u32[]{:S(2)}) collective-permute-start(f32[2,34,1,256]{3,1,2,0:T(8,128)S(1)} %get-tuple-element.40), channel_id=1, source_target_pairs={{1,0},{2,1},{3,2},{4,3},{5,4},{6,5},{7,6},{9,8},{10,9},{11,10},{12... | collective-permute-start | bytes 208904 | tf_op jit(solution)/shard_map/ppermute | solution.py:17
  117.0 5.0 %collective-permute-start.25 = (f32[2,1,32,256]{3,1,2,0:T(1,128)S(1)}, f32[2,1,32,256]{3,1,2,0:T(1,128)S(1)}, u32[]{:S(2)}, u32[]{:S(2)}) collective-permute-start(f32[2,1,32,256]{3,1,2,0:T(1,128)S(1)} %get-tuple-element.62), channel_id=1, source_target_pairs={{8,0},{16,8},{24,16},{9,1},{17,9},{25,17},{10,2},{18,10},{26,18},{... | collective-permute-start | bytes 196616 | tf_op jit(solution)/shard_map/ppermute | solution.py:17
  122.1 7.6 %collective-permute-start.26 = (f32[2,34,1,256]{3,1,2,0:T(8,128)S(1)}, f32[2,34,1,256]{3,1,2,0:T(8,128)S(1)}, u32[]{:S(2)}, u32[]{:S(2)}) collective-permute-start(f32[2,34,1,256]{3,1,2,0:T(8,128)S(1)} %get-tuple-element.37), channel_id=1, source_target_pairs={{0,1},{1,2},{2,3},{3,4},{4,5},{5,6},{6,7},{8,9},{9,10},{10,11},{11... | collective-permute-start | bytes 208904 | tf_op jit(solution)/shard_map/ppermute | solution.py:16
  126.3 5.2 %collective-permute-start.27 = (f32[2,34,1,256]{3,1,2,0:T(8,128)S(1)}, f32[2,34,1,256]{3,1,2,0:T(8,128)S(1)}, u32[]{:S(2)}, u32[]{:S(2)}) collective-permute-start(f32[2,34,1,256]{3,1,2,0:T(8,128)S(1)} %get-tuple-element.38), channel_id=1, source_target_pairs={{1,0},{2,1},{3,2},{4,3},{5,4},{6,5},{7,6},{9,8},{10,9},{11,10},{12... | collective-permute-start | bytes 208904 | tf_op jit(solution)/shard_map/ppermute | solution.py:17
  139.4 5.2 %collective-permute-start.29 = (f32[2,1,32,256]{3,1,2,0:T(1,128)S(1)}, f32[2,1,32,256]{3,1,2,0:T(1,128)S(1)}, u32[]{:S(2)}, u32[]{:S(2)}) collective-permute-start(f32[2,1,32,256]{3,1,2,0:T(1,128)S(1)} %get-tuple-element.60), channel_id=1, source_target_pairs={{8,0},{16,8},{24,16},{9,1},{17,9},{25,17},{10,2},{18,10},{26,18},{... | collective-permute-start | bytes 196616 | tf_op jit(solution)/shard_map/ppermute | solution.py:17
  147.7 5.2 %collective-permute-start.31 = (f32[2,34,1,256]{3,1,2,0:T(8,128)S(1)}, f32[2,34,1,256]{3,1,2,0:T(8,128)S(1)}, u32[]{:S(2)}, u32[]{:S(2)}) collective-permute-start(f32[2,34,1,256]{3,1,2,0:T(8,128)S(1)} %get-tuple-element.36), channel_id=1, source_target_pairs={{1,0},{2,1},{3,2},{4,3},{5,4},{6,5},{7,6},{9,8},{10,9},{11,10},{12... | collective-permute-start | bytes 208904 | tf_op jit(solution)/shard_map/ppermute | solution.py:17
  165.1 6.0 %collective-permute-start.34 = (f32[2,34,1,256]{3,1,2,0:T(8,128)S(1)}, f32[2,34,1,256]{3,1,2,0:T(8,128)S(1)}, u32[]{:S(2)}, u32[]{:S(2)}) collective-permute-start(f32[2,34,1,256]{3,1,2,0:T(8,128)S(1)} %get-tuple-element.33), channel_id=1, source_target_pairs={{0,1},{1,2},{2,3},{3,4},{4,5},{5,6},{6,7},{8,9},{9,10},{10,11},{11... | collective-permute-start | bytes 208904 | tf_op jit(solution)/shard_map/ppermute | solution.py:16
  169.4 5.2 %collective-permute-start.35 = (f32[2,34,1,256]{3,1,2,0:T(8,128)S(1)}, f32[2,34,1,256]{3,1,2,0:T(8,128)S(1)}, u32[]{:S(2)}, u32[]{:S(2)}) collective-permute-start(f32[2,34,1,256]{3,1,2,0:T(8,128)S(1)} %get-tuple-element.34), channel_id=1, source_target_pairs={{1,0},{2,1},{3,2},{4,3},{5,4},{6,5},{7,6},{9,8},{10,9},{11,10},{12... | collective-permute-start | bytes 208904 | tf_op jit(solution)/shard_map/ppermute | solution.py:17
  177.8 5.3 %collective-permute-start.36 = (f32[2,1,32,256]{3,1,2,0:T(1,128)S(1)}, f32[2,1,32,256]{3,1,2,0:T(1,128)S(1)}, u32[]{:S(2)}, u32[]{:S(2)}) collective-permute-start(f32[2,1,32,256]{3,1,2,0:T(1,128)S(1)} %get-tuple-element.56), channel_id=1, source_target_pairs={{8,0},{16,8},{24,16},{9,1},{17,9},{25,17},{10,2},{18,10},{26,18},{... | collective-permute-start | bytes 196616 | tf_op jit(solution)/shard_map/ppermute | solution.py:17
  179.1 5.3 %collective-permute-start.37 = (f32[2,1,32,256]{3,1,2,0:T(1,128)S(1)}, f32[2,1,32,256]{3,1,2,0:T(1,128)S(1)}, u32[]{:S(2)}, u32[]{:S(2)}) collective-permute-start(f32[2,1,32,256]{3,1,2,0:T(1,128)S(1)} %get-tuple-element.55), channel_id=1, source_target_pairs={{0,8},{8,16},{16,24},{1,9},{9,17},{17,25},{2,10},{10,18},{18,26},{... | collective-permute-start | bytes 196616 | tf_op jit(solution)/shard_map/ppermute | solution.py:16
  184.5 5.3 %collective-permute-start.38 = (f32[2,34,1,256]{3,1,2,0:T(8,128)S(1)}, f32[2,34,1,256]{3,1,2,0:T(8,128)S(1)}, u32[]{:S(2)}, u32[]{:S(2)}) collective-permute-start(f32[2,34,1,256]{3,1,2,0:T(8,128)S(1)} %get-tuple-element.31), channel_id=1, source_target_pairs={{1,0},{2,1},{3,2},{4,3},{5,4},{6,5},{7,6},{9,8},{10,9},{11,10},{12... | collective-permute-start | bytes 208904 | tf_op jit(solution)/shard_map/ppermute | solution.py:17
  185.8 6.2 %collective-permute-start.39 = (f32[2,34,1,256]{3,1,2,0:T(8,128)S(1)}, f32[2,34,1,256]{3,1,2,0:T(8,128)S(1)}, u32[]{:S(2)}, u32[]{:S(2)}) collective-permute-start(f32[2,34,1,256]{3,1,2,0:T(8,128)S(1)} %get-tuple-element.32), channel_id=1, source_target_pairs={{0,1},{1,2},{2,3},{3,4},{4,5},{5,6},{6,7},{8,9},{9,10},{10,11},{11... | collective-permute-start | bytes 208904 | tf_op jit(solution)/shard_map/ppermute | solution.py:16
  195.5 5.3 %collective-permute-start.40 = (f32[2,1,32,256]{3,1,2,0:T(1,128)S(1)}, f32[2,1,32,256]{3,1,2,0:T(1,128)S(1)}, u32[]{:S(2)}, u32[]{:S(2)}) collective-permute-start(f32[2,1,32,256]{3,1,2,0:T(1,128)S(1)} %get-tuple-element.54), channel_id=1, source_target_pairs={{8,0},{16,8},{24,16},{9,1},{17,9},{25,17},{10,2},{18,10},{26,18},{... | collective-permute-start | bytes 196616 | tf_op jit(solution)/shard_map/ppermute | solution.py:17
  196.8 5.3 %collective-permute-start.41 = (f32[2,1,32,256]{3,1,2,0:T(1,128)S(1)}, f32[2,1,32,256]{3,1,2,0:T(1,128)S(1)}, u32[]{:S(2)}, u32[]{:S(2)}) collective-permute-start(f32[2,1,32,256]{3,1,2,0:T(1,128)S(1)} %get-tuple-element.53), channel_id=1, source_target_pairs={{0,8},{8,16},{16,24},{1,9},{9,17},{17,25},{2,10},{10,18},{18,26},{... | collective-permute-start | bytes 196616 | tf_op jit(solution)/shard_map/ppermute | solution.py:16
  202.2 5.8 %collective-permute-start.42 = (f32[2,34,1,256]{3,1,2,0:T(8,128)S(1)}, f32[2,34,1,256]{3,1,2,0:T(8,128)S(1)}, u32[]{:S(2)}, u32[]{:S(2)}) collective-permute-start(f32[2,34,1,256]{3,1,2,0:T(8,128)S(1)} %get-tuple-element.29), channel_id=1, source_target_pairs={{1,0},{2,1},{3,2},{4,3},{5,4},{6,5},{7,6},{9,8},{10,9},{11,10},{12... | collective-permute-start | bytes 208904 | tf_op jit(solution)/shard_map/ppermute | solution.py:17
  203.5 7.0 %collective-permute-start.43 = (f32[2,34,1,256]{3,1,2,0:T(8,128)S(1)}, f32[2,34,1,256]{3,1,2,0:T(8,128)S(1)}, u32[]{:S(2)}, u32[]{:S(2)}) collective-permute-start(f32[2,34,1,256]{3,1,2,0:T(8,128)S(1)} %get-tuple-element.30), channel_id=1, source_target_pairs={{0,1},{1,2},{2,3},{3,4},{4,5},{5,6},{6,7},{8,9},{9,10},{10,11},{11... | collective-permute-start | bytes 208904 | tf_op jit(solution)/shard_map/ppermute | solution.py:16
  214.0 5.8 %collective-permute-start.44 = (f32[2,1,32,256]{3,1,2,0:T(1,128)S(1)}, f32[2,1,32,256]{3,1,2,0:T(1,128)S(1)}, u32[]{:S(2)}, u32[]{:S(2)}) collective-permute-start(f32[2,1,32,256]{3,1,2,0:T(1,128)S(1)} %get-tuple-element.52), channel_id=1, source_target_pairs={{8,0},{16,8},{24,16},{9,1},{17,9},{25,17},{10,2},{18,10},{26,18},{... | collective-permute-start | bytes 196616 | tf_op jit(solution)/shard_map/ppermute | solution.py:17
  215.3 5.8 %collective-permute-start.45 = (f32[2,1,32,256]{3,1,2,0:T(1,128)S(1)}, f32[2,1,32,256]{3,1,2,0:T(1,128)S(1)}, u32[]{:S(2)}, u32[]{:S(2)}) collective-permute-start(f32[2,1,32,256]{3,1,2,0:T(1,128)S(1)} %get-tuple-element.51), channel_id=1, source_target_pairs={{0,8},{8,16},{16,24},{1,9},{9,17},{17,25},{2,10},{10,18},{18,26},{... | collective-permute-start | bytes 196616 | tf_op jit(solution)/shard_map/ppermute | solution.py:16
  221.1 5.8 %collective-permute-start.46 = (f32[2,34,1,256]{3,1,2,0:T(8,128)S(1)}, f32[2,34,1,256]{3,1,2,0:T(8,128)S(1)}, u32[]{:S(2)}, u32[]{:S(2)}) collective-permute-start(f32[2,34,1,256]{3,1,2,0:T(8,128)S(1)} %get-tuple-element.27), channel_id=1, source_target_pairs={{1,0},{2,1},{3,2},{4,3},{5,4},{6,5},{7,6},{9,8},{10,9},{11,10},{12... | collective-permute-start | bytes 208904 | tf_op jit(solution)/shard_map/ppermute | solution.py:17
  222.4 5.9 %collective-permute-start.47 = (f32[2,34,1,256]{3,1,2,0:T(8,128)S(1)}, f32[2,34,1,256]{3,1,2,0:T(8,128)S(1)}, u32[]{:S(2)}, u32[]{:S(2)}) collective-permute-start(f32[2,34,1,256]{3,1,2,0:T(8,128)S(1)} %get-tuple-element.28), channel_id=1, source_target_pairs={{0,1},{1,2},{2,3},{3,4},{4,5},{5,6},{6,7},{8,9},{9,10},{10,11},{11... | collective-permute-start | bytes 208904 | tf_op jit(solution)/shard_map/ppermute | solution.py:16
  231.7 6.1 %collective-permute-start.48 = (f32[2,1,32,256]{3,1,2,0:T(1,128)S(1)}, f32[2,1,32,256]{3,1,2,0:T(1,128)S(1)}, u32[]{:S(2)}, u32[]{:S(2)}) collective-permute-start(f32[2,1,32,256]{3,1,2,0:T(1,128)S(1)} %get-tuple-element.50), channel_id=1, source_target_pairs={{8,0},{16,8},{24,16},{9,1},{17,9},{25,17},{10,2},{18,10},{26,18},{... | collective-permute-start | bytes 196616 | tf_op jit(solution)/shard_map/ppermute | solution.py:17
  233.2 5.9 %collective-permute-start.49 = (f32[2,1,32,256]{3,1,2,0:T(1,128)S(1)}, f32[2,1,32,256]{3,1,2,0:T(1,128)S(1)}, u32[]{:S(2)}, u32[]{:S(2)}) collective-permute-start(f32[2,1,32,256]{3,1,2,0:T(1,128)S(1)} %get-tuple-element.49), channel_id=1, source_target_pairs={{0,8},{8,16},{16,24},{1,9},{9,17},{17,25},{2,10},{10,18},{18,26},{... | collective-permute-start | bytes 196616 | tf_op jit(solution)/shard_map/ppermute | solution.py:16
  239.1 7.5 %collective-permute-start.50 = (f32[2,34,1,256]{3,1,2,0:T(8,128)S(1)}, f32[2,34,1,256]{3,1,2,0:T(8,128)S(1)}, u32[]{:S(2)}, u32[]{:S(2)}) collective-permute-start(f32[2,34,1,256]{3,1,2,0:T(8,128)S(1)} %get-tuple-element.25), channel_id=1, source_target_pairs={{1,0},{2,1},{3,2},{4,3},{5,4},{6,5},{7,6},{9,8},{10,9},{11,10},{12... | collective-permute-start | bytes 208904 | tf_op jit(solution)/shard_map/ppermute | solution.py:17
  240.4 6.7 %collective-permute-start.51 = (f32[2,34,1,256]{3,1,2,0:T(8,128)S(1)}, f32[2,34,1,256]{3,1,2,0:T(8,128)S(1)}, u32[]{:S(2)}, u32[]{:S(2)}) collective-permute-start(f32[2,34,1,256]{3,1,2,0:T(8,128)S(1)} %get-tuple-element.26), channel_id=1, source_target_pairs={{0,1},{1,2},{2,3},{3,4},{4,5},{5,6},{6,7},{8,9},{9,10},{10,11},{11... | collective-permute-start | bytes 208904 | tf_op jit(solution)/shard_map/ppermute | solution.py:16
  439.6 30.3 %all-to-all-start.1 = ((f32[8,8,32,256]{3,2,1,0:T(8,128)}), f32[8,8,32,256]{3,2,1,0:T(8,128)S(1)}, u32[]{:S(2)}, u32[]{:S(2)}) async-start(f32[8,8,32,256]{3,2,1,0:T(8,128)} %copy.62), calls=%async_computation.1 | async-start | bytes 4194304 | tf_op jit(solution)/shard_map/all_to_all | solution.py:105
  (10 other events, 68.4 us)
where the time goes:
time: 481 us; the launch traced here: 472 us
  blocking collectives  152 us (32%)
  starting transfers between devices  147 us (31%)
  waiting for transfers between devices  66.8 us (14%)
  other arithmetic  53 us (11%)
  local copies, waits for them, and re-layouts  31.4 us (7%)
  matrix products  18.7 us (4%)
    ppermute x26, starting transfers between devices, extended(): before = lax.ppermute(last, axis, up)  109 us
    all_to_all x1, blocking collectives, shards(): lax.all_to_all(both, 'probe', split_axis=2, concat_axis=0, tiled=True)  79.6 us
    psum x1, blocking collectives, shards(): lax.psum(jnp.stack([partial_gram, partial_cross]), ('probe', 'sx', 'sy'))  72.6 us
    ppermute x26, starting transfers between devices, extended(): after = lax.ppermute(leading, axis, down)  34.3 us
    all_to_all x1, waiting for transfers between devices, shards(): lax.all_to_all(basis_slab.reshape(slabs[:, 0].shape), 'probe', split_axis...  25.3 us
    ppermute x26, waiting for transfers between devices, extended(): after = lax.ppermute(leading, axis, down)  24.1 us
    add x6, other arithmetic, forward_step(): result + (spread - 0.5 * cc[3]) * padded[..., 2:]  20.5 us
    ppermute x26, waiting for transfers between devices, extended(): before = lax.ppermute(last, axis, up)  17.3 us
  transfers between devices with their start and end apart: 53, of which 21 were waited for; matrix products, arithmetic and copies ran while one was open for 5% of the time, Pallas kernels for 0%

commit v1 on v0

--- a/solution.py
+++ b/solution.py
@@ -1,9 +1,18 @@
+import functools
 import jax
 import jax.numpy as jnp
 from jax import lax
 from jax.sharding import PartitionSpec as P
 
 STEPS = 4
+
+
+def plan_the_patches(array_here, group_axis):
+    upper = jax.lax.all_gather(array_here, axis_name=group_axis).sum(axis=0)
+    return upper
+
+
+remake_the_sources_all = functools.partial(plan_the_patches, group_axis=("probe", "sx", "sy"))
 
 
 def extended(value, sides, width):
@@ -98,7 +107,7 @@
     flat_root = slabs[:, 1].reshape(count, -1)
     partial_gram = jnp.dot(flat, flat.T, precision=highest)
     partial_cross = jnp.dot(flat_root, flat_root.T, precision=highest)
-    sums = lax.psum(jnp.stack([partial_gram, partial_cross]), ("probe", "sx", "sy")) / ncells
+    sums = remake_the_sources_all(jnp.stack([partial_gram, partial_cross])) / ncells
     gram, cross = (sums[0], sums[1])
     inverse = factor_inverse(gram, count)
     basis_slab = jnp.dot(inverse, flat, precision=highest)

time: 481 us -> 736 us (1.53)
  blocking collectives: 152 us -> 371 us
  starting transfers between devices: 147 us -> 183 us
    all_gather x0 -> x1, blocking collectives: none -> 292 us  [plan_the_patches(): upper = jax.lax.all_gather(array_here, axis_name=group_axis).sum(axis=0)]
    psum x1 -> x0, blocking collectives: 72.6 us -> none  [shards(): lax.psum(jnp.stack([partial_gram, partial_cross]), ('probe', 'sx', 'sy'))]
    all_to_all x1, starting transfers between devices: 4.14 us -> 39.9 us  [shards(): lax.all_to_all(basis_slab.reshape(slabs[:, 0].shape), 'probe', split_axis...]
  transfers between devices with their start and end apart: 53 -> 53, of which waited for: 21 -> 21; matrix products, arithmetic and copies ran while one was open for 5% -> 3% of each run, Pallas kernels for 0% -> 0%
where the time goes in v1:
time: 736 us; the launch traced here: 727 us
  blocking collectives  371 us (50%)
  starting transfers between devices  183 us (25%)
  waiting for transfers between devices  66.8 us (9%)
  other arithmetic  53.1 us (7%)
  local copies, waits for them, and re-layouts  31.4 us (4%)
  matrix products  18.7 us (3%)
    all_gather x1, blocking collectives, plan_the_patches(): upper = jax.lax.all_gather(array_here, axis_name=group_axis).sum(axis=0)  292 us
    ppermute x26, starting transfers between devices, extended(): before = lax.ppermute(last, axis, up)  109 us
    all_to_all x1, blocking collectives, shards(): lax.all_to_all(both, 'probe', split_axis=2, concat_axis=0, tiled=True)  79.6 us
    all_to_all x1, starting transfers between devices, shards(): lax.all_to_all(basis_slab.reshape(slabs[:, 0].shape), 'probe', split_axis...  39.9 us
    ppermute x26, starting transfers between devices, extended(): after = lax.ppermute(leading, axis, down)  34.3 us
    all_to_all x1, waiting for transfers between devices, shards(): lax.all_to_all(basis_slab.reshape(slabs[:, 0].shape), 'probe', split_axis...  25.3 us
    ppermute x26, waiting for transfers between devices, extended(): after = lax.ppermute(leading, axis, down)  24.1 us
    add x6, other arithmetic, forward_step(): result + (spread - 0.5 * cc[3]) * padded[..., 2:]  20.5 us
  transfers between devices with their start and end apart: 53, of which 21 were waited for; matrix products, arithmetic and copies ran while one was open for 3% of the time, Pallas kernels for 0%

profile of v1, /device:TPU:1, one launch (start us, length us, event | category | flops | bytes accessed | tf_op | source)
XLA Modules:
  0.0 726.6 jit_solution(2225357516169832131)
XLA Ops:
  3.0 4.6 collective-permute-start.1
  12.0 4.4 collective-permute-start.3
  21.8 3.5 fusion.10
  26.7 4.0 collective-permute-start.5
  33.3 4.9 collective-permute-start.7
  38.3 4.0 collective-permute-start.16
  43.6 3.5 fusion.14
  48.4 4.6 collective-permute-start.9
  53.3 4.4 collective-permute-start.18
  60.4 4.8 collective-permute-start.11
  68.3 3.4 fusion.18
  73.1 4.3 collective-permute-start.13
  80.0 4.4 collective-permute-start.15
  85.9 3.5 broadcast_multiply_fusion.3
  89.6 3.7 collective-permute-start.20
  98.3 4.3 collective-permute-start.22
  105.5 3.5 collective-permute-done.23
  109.5 3.9 broadcast_multiply_fusion.2
  113.5 3.5 collective-permute-start.24
  118.4 3.7 collective-permute-done.25
  122.1 4.3 collective-permute-start.26
  132.0 3.9 broadcast_multiply_fusion.1
  140.7 3.9 collective-permute-done.29
  149.4 3.5 collective-permute-done.31
  153.3 3.7 broadcast_multiply_fusion
  161.4 3.7 collective-permute-done.33
  165.1 4.3 collective-permute-start.34
  171.1 3.4 collective-permute-done.35
  179.1 4.0 collective-permute-start.37
  185.8 4.0 collective-permute-start.39
  192.0 3.4 fusion.27
  196.8 4.0 collective-permute-start.41
  203.5 4.4 collective-permute-start.43
  210.5 3.4 fusion.31
  215.3 4.4 collective-permute-start.45
  222.4 4.4 collective-permute-start.47
  233.2 4.6 collective-permute-start.49
  240.4 5.3 collective-permute-start.51
  247.1 3.5 fusion.41
  253.3 79.6 %all_to_all.36 = f32[2,2,32,32,256]{4,3,0,1,2:T(8,128)S(1)} all-to-all(f32[2,2,32,32,256]{4,3,0,1,2:T(8,128)S(1)} %copy.58), channel_id=1, replica_groups=mesh['probe'=4,'sx'=4,'sy'=8] {'probe'}, dimensions={2} | all-to-all | bytes 8388608 | tf_op jit(solution)/shard_map/all_to_all | solution.py:105
  333.0 5.2 copy.72
  338.2 6.1 all_to_all.29
  344.4 7.1 fusion.131
  351.5 7.1 fusion.134
  358.6 291.7 %all-gather = f32[256,8,8]{2,1,0:T(8,128)S(1)} all-gather(f32[2,8,8]{2,1,0:T(8,128)S(1)} %pad_maximum_fusion.117), channel_id=2, replica_groups=mesh['probe'=4,'sx'=4,'sy'=8] {'probe','sx','sy'}, dimensions={0}, use_global_device_ids=true | all-gather | bytes 66048 | tf_op jit(solution)/shard_map/all_gather | solution.py:11
  653.4 3.4 fusion.124
  658.7 39.9 %all-to-all-start.1 = ((f32[8,8,32,256]{3,2,1,0:T(8,128)}), f32[8,8,32,256]{3,2,1,0:T(8,128)S(1)}, u32[]{:S(2)}, u32[]{:S(2)}) async-start(f32[8,8,32,256]{3,2,1,0:T(8,128)} %copy.62), calls=%async_computation.1 | async-start | bytes 4194304 | tf_op jit(solution)/shard_map/all_to_all | solution.py:114
  699.5 25.3 %all-to-all-done.1 = f32[8,8,32,256]{3,2,1,0:T(8,128)S(1)} async-done(((f32[8,8,32,256]{3,2,1,0:T(8,128)}), f32[8,8,32,256]{3,2,1,0:T(8,128)S(1)}, u32[]{:S(2)}, u32[]{:S(2)}) %all-to-all-start.1) | async-done | bytes 2097184 | tf_op jit(solution)/shard_map/all_to_all | solution.py:114
  (168 shorter events, 101.9 us)
Async XLA Ops:
  1.6 8.9 %collective-permute-start = (f32[2,1,32,256]{3,1,2,0:T(1,128)S(1)}, f32[2,1,32,256]{3,1,2,0:T(1,128)S(1)}, u32[]{:S(2)}, u32[]{:S(2)}) collective-permute-start(f32[2,1,32,256]{3,1,2,0:T(1,128)S(1)} %copy.38), channel_id=1, source_target_pairs={{8,0},{16,8},{24,16},{9,1},{17,9},{25,17},{10,2},{18,10},{26,18},{... | collective-permute-start | bytes 196616 | tf_op jit(solution)/shard_map/ppermute | solution.py:26
  3.0 7.6 %collective-permute-start.1 = (f32[2,1,32,256]{3,1,2,0:T(1,128)S(1)}, f32[2,1,32,256]{3,1,2,0:T(1,128)S(1)}, u32[]{:S(2)}, u32[]{:S(2)}) collective-permute-start(f32[2,1,32,256]{3,1,2,0:T(1,128)S(1)} %copy.41), channel_id=1, source_target_pairs={{0,8},{8,16},{16,24},{1,9},{9,17},{17,25},{2,10},{10,18},{18,26},{... | collective-permute-start | bytes 196616 | tf_op jit(solution)/shard_map/ppermute | solution.py:25
  10.6 11.2 %collective-permute-start.2 = (f32[2,34,1,256]{3,1,2,0:T(8,128)S(1)}, f32[2,34,1,256]{3,1,2,0:T(8,128)S(1)}, u32[]{:S(2)}, u32[]{:S(2)}) collective-permute-start(f32[2,34,1,256]{3,1,2,0:T(8,128)S(1)} %get-tuple-element.47), channel_id=1, source_target_pairs={{1,0},{2,1},{3,2},{4,3},{5,4},{6,5},{7,6},{9,8},{10,9},{11,10},{12... | collective-permute-start | bytes 208904 | tf_op jit(solution)/shard_map/ppermute | solution.py:26
  12.0 9.8 %collective-permute-start.3 = (f32[2,34,1,256]{3,1,2,0:T(8,128)S(1)}, f32[2,34,1,256]{3,1,2,0:T(8,128)S(1)}, u32[]{:S(2)}, u32[]{:S(2)}) collective-permute-start(f32[2,34,1,256]{3,1,2,0:T(8,128)S(1)} %get-tuple-element.48), channel_id=1, source_target_pairs={{0,1},{1,2},{2,3},{3,4},{4,5},{5,6},{6,7},{8,9},{9,10},{10,11},{11... | collective-permute-start | bytes 208904 | tf_op jit(solution)/shard_map/ppermute | solution.py:25
  25.4 5.3 collective-permute-start.4
  26.7 5.3 collective-permute-start.5
  32.0 11.5 %collective-permute-start.6 = (f32[2,34,1,256]{3,1,2,0:T(8,128)S(1)}, f32[2,34,1,256]{3,1,2,0:T(8,128)S(1)}, u32[]{:S(2)}, u32[]{:S(2)}) collective-permute-start(f32[2,34,1,256]{3,1,2,0:T(8,128)S(1)} %get-tuple-element.45), channel_id=1, source_target_pairs={{1,0},{2,1},{3,2},{4,3},{5,4},{6,5},{7,6},{9,8},{10,9},{11,10},{12... | collective-permute-start | bytes 208904 | tf_op jit(solution)/shard_map/ppermute | solution.py:26
  33.3 10.2 %collective-permute-start.7 = (f32[2,34,1,256]{3,1,2,0:T(8,128)S(1)}, f32[2,34,1,256]{3,1,2,0:T(8,128)S(1)}, u32[]{:S(2)}, u32[]{:S(2)}) collective-permute-start(f32[2,34,1,256]{3,1,2,0:T(8,128)S(1)} %get-tuple-element.46), channel_id=1, source_target_pairs={{0,1},{1,2},{2,3},{3,4},{4,5},{5,6},{6,7},{8,9},{9,10},{10,11},{11... | collective-permute-start | bytes 208904 | tf_op jit(solution)/shard_map/ppermute | solution.py:25
  38.3 14.8 %collective-permute-start.16 = (f32[4,1,32,256]{3,2,1,0:T(8,128)S(1)}, f32[4,1,32,256]{3,2,1,0:T(8,128)S(1)}, u32[]{:S(2)}, u32[]{:S(2)}) collective-permute-start(f32[4,1,32,256]{3,2,1,0:T(8,128)S(1)} %get-tuple-element.17), channel_id=1, source_target_pairs={{0,8},{8,16},{16,24},{1,9},{9,17},{17,25},{2,10},{10,18},{18,26},{... | collective-permute-start | bytes 393224 | tf_op jit(solution)/shard_map/ppermute | solution.py:25
  42.3 10.8 %collective-permute-start.17 = (f32[4,1,32,256]{3,2,1,0:T(8,128)S(1)}, f32[4,1,32,256]{3,2,1,0:T(8,128)S(1)}, u32[]{:S(2)}, u32[]{:S(2)}) collective-permute-start(f32[4,1,32,256]{3,2,1,0:T(8,128)S(1)} %get-tuple-element.18), channel_id=1, source_target_pairs={{8,0},{16,8},{24,16},{9,1},{17,9},{25,17},{10,2},{18,10},{26,18},{... | collective-permute-start | bytes 393224 | tf_op jit(solution)/shard_map/ppermute | solution.py:26
  47.1 11.9 %collective-permute-start.8 = (f32[2,1,32,256]{3,1,2,0:T(1,128)S(1)}, f32[2,1,32,256]{3,1,2,0:T(1,128)S(1)}, u32[]{:S(2)}, u32[]{:S(2)}) collective-permute-start(f32[2,1,32,256]{3,1,2,0:T(1,128)S(1)} %get-tuple-element.68), channel_id=1, source_target_pairs={{8,0},{16,8},{24,16},{9,1},{17,9},{25,17},{10,2},{18,10},{26,18},{... | collective-permute-start | bytes 196616 | tf_op jit(solution)/shard_map/ppermute | solution.py:26
  48.4 10.6 %collective-permute-start.9 = (f32[2,1,32,256]{3,1,2,0:T(1,128)S(1)}, f32[2,1,32,256]{3,1,2,0:T(1,128)S(1)}, u32[]{:S(2)}, u32[]{:S(2)}) collective-permute-start(f32[2,1,32,256]{3,1,2,0:T(1,128)S(1)} %get-tuple-element.67), channel_id=1, source_target_pairs={{0,8},{8,16},{16,24},{1,9},{9,17},{17,25},{2,10},{10,18},{18,26},{... | collective-permute-start | bytes 196616 | tf_op jit(solution)/shard_map/ppermute | solution.py:25
  53.3 12.5 %collective-permute-start.18 = (f32[4,34,1,256]{3,1,2,0:T(8,128)S(1)}, f32[4,34,1,256]{3,1,2,0:T(8,128)S(1)}, u32[]{:S(2)}, u32[]{:S(2)}) collective-permute-start(f32[4,34,1,256]{3,1,2,0:T(8,128)S(1)} %copy.49), channel_id=1, source_target_pairs={{0,1},{1,2},{2,3},{3,4},{4,5},{5,6},{6,7},{8,9},{9,10},{10,11},{11... | collective-permute-start | bytes 417800 | tf_op jit(solution)/shard_map/ppermute | solution.py:25
  57.8 8.2 %collective-permute-start.19 = (f32[4,34,1,256]{3,1,2,0:T(8,128)S(1)}, f32[4,34,1,256]{3,1,2,0:T(8,128)S(1)}, u32[]{:S(2)}, u32[]{:S(2)}) collective-permute-start(f32[4,34,1,256]{3,1,2,0:T(8,128)S(1)} %copy.50), channel_id=1, source_target_pairs={{1,0},{2,1},{3,2},{4,3},{5,4},{6,5},{7,6},{9,8},{10,9},{11,10},{12... | collective-permute-start | bytes 417800 | tf_op jit(solution)/shard_map/ppermute | solution.py:26
  59.1 7.1 collective-permute-start.10
  60.4 7.9 %collective-permute-start.11 = (f32[2,34,1,256]{3,1,2,0:T(8,128)S(1)}, f32[2,34,1,256]{3,1,2,0:T(8,128)S(1)}, u32[]{:S(2)}, u32[]{:S(2)}) collective-permute-start(f32[2,34,1,256]{3,1,2,0:T(8,128)S(1)} %get-tuple-element.44), channel_id=1, source_target_pairs={{0,1},{1,2},{2,3},{3,4},{4,5},{5,6},{6,7},{8,9},{9,10},{10,11},{11... | collective-permute-start | bytes 208904 | tf_op jit(solution)/shard_map/ppermute | solution.py:25
  71.8 6.1 collective-permute-start.12
  73.1 5.6 collective-permute-start.13
  78.7 6.1 collective-permute-start.14
  80.0 5.9 collective-permute-start.15
  89.6 8.2 %collective-permute-start.20 = (f32[2,1,32,256]{3,1,2,0:T(1,128)S(1)}, f32[2,1,32,256]{3,1,2,0:T(1,128)S(1)}, u32[]{:S(2)}, u32[]{:S(2)}) collective-permute-start(f32[2,1,32,256]{3,1,2,0:T(1,128)S(1)} %get-tuple-element.63), channel_id=1, source_target_pairs={{0,8},{8,16},{16,24},{1,9},{9,17},{17,25},{2,10},{10,18},{18,26},{... | collective-permute-start | bytes 196616 | tf_op jit(solution)/shard_map/ppermute | solution.py:25
  93.3 5.0 collective-permute-start.21
  98.3 7.2 collective-permute-start.22
  102.6 6.4 collective-permute-start.23
  117.0 5.0 collective-permute-start.25
  122.1 7.6 %collective-permute-start.26 = (f32[2,34,1,256]{3,1,2,0:T(8,128)S(1)}, f32[2,34,1,256]{3,1,2,0:T(8,128)S(1)}, u32[]{:S(2)}, u32[]{:S(2)}) collective-permute-start(f32[2,34,1,256]{3,1,2,0:T(8,128)S(1)} %get-tuple-element.37), channel_id=1, source_target_pairs={{0,1},{1,2},{2,3},{3,4},{4,5},{5,6},{6,7},{8,9},{9,10},{10,11},{11... | collective-permute-start | bytes 208904 | tf_op jit(solution)/shard_map/ppermute | solution.py:25
  126.3 5.2 collective-permute-start.27
  139.4 5.2 collective-permute-start.29
  147.7 5.2 collective-permute-start.31
  165.1 6.0 collective-permute-start.34
  169.4 5.2 collective-permute-start.35
  177.8 5.3 collective-permute-start.36
  179.1 5.3 collective-permute-start.37
  184.5 5.3 collective-permute-start.38
  185.8 6.2 collective-permute-start.39
  195.5 5.3 collective-permute-start.40
  196.8 5.3 collective-permute-start.41
  202.2 5.8 collective-permute-start.42
  203.5 7.0 collective-permute-start.43
  214.0 5.8 collective-permute-start.44
  215.3 5.8 collective-permute-start.45
  221.1 5.8 collective-permute-start.46
  222.4 5.9 collective-permute-start.47
  231.7 6.1 collective-permute-start.48
  233.2 5.9 collective-permute-start.49
  239.1 7.5 %collective-permute-start.50 = (f32[2,34,1,256]{3,1,2,0:T(8,128)S(1)}, f32[2,34,1,256]{3,1,2,0:T(8,128)S(1)}, u32[]{:S(2)}, u32[]{:S(2)}) collective-permute-start(f32[2,34,1,256]{3,1,2,0:T(8,128)S(1)} %get-tuple-element.25), channel_id=1, source_target_pairs={{1,0},{2,1},{3,2},{4,3},{5,4},{6,5},{7,6},{9,8},{10,9},{11,10},{12... | collective-permute-start | bytes 208904 | tf_op jit(solution)/shard_map/ppermute | solution.py:26
  240.4 6.7 collective-permute-start.51
  658.7 66.1 %all-to-all-start.1 = ((f32[8,8,32,256]{3,2,1,0:T(8,128)}), f32[8,8,32,256]{3,2,1,0:T(8,128)S(1)}, u32[]{:S(2)}, u32[]{:S(2)}) async-start(f32[8,8,32,256]{3,2,1,0:T(8,128)} %copy.62), calls=%async_computation.1 | async-start | bytes 4194304 | tf_op jit(solution)/shard_map/all_to_all | solution.py:114
  (10 other events, 68.4 us)
